TPU v7x, 32 devices: a whole 2x2x4 slice. The times are simulated.
32 devices in a mesh: dp: 2 (over y), table: 16 (over z, x, core).
Axes of the slice: x: 2, y: 2, z: 4, core: 2. Of those that a mesh axis runs over, the one named last changes fastest.
Arguments:
- gradients: bfloat16 [256, 4096], P(None, ('dp', 'table')), may hold values from -16 to 16
- row_ids: int32 [4096], P(('dp', 'table')), may hold values from 0 to 32767
- table_block: float32 [256, 32768], P('table', 'dp'), may hold values from -6 to 6
- adagrad_state: float32 [32768], P('dp'), may hold values from 0.05 to 2
Outputs:
- new_table: float32 [256, 32768], P('table', 'dp')
- new_state: float32 [32768], P('dp')
All inputs are finite; a program needn't handle non-finite values.
Results may differ from a plain program's by a relative error of at most 0.0003.
Values may be sent and summed in bfloat16 or wider, within the bound.
A program may use at most 64 MiB of HBM per device.

v0:
```python
import jax
import jax.numpy as jnp
from jax import lax
from jax.sharding import PartitionSpec as P

W = 256
learn_rate = 0.5


def accumulate(grads, ids, first_row, count_rows):
    relative = ids - first_row
    inside = (relative >= 0) & (relative < count_rows)
    target = jnp.where(inside, relative, count_rows)
    start_total = jnp.zeros((grads.shape[0], count_rows), jnp.float32)
    return start_total.at[:, target].add(grads.astype(jnp.float32), mode="drop")


def body(gradients, row_ids, table_block, adagrad_state):
    owned = lax.all_to_all(gradients, "table", split_axis=0, concat_axis=1, tiled=True)
    local_rows = table_block.shape[1]
    all_row_ids = lax.all_gather(row_ids, ("dp", "table"), axis=0, tiled=True)
    first_row = lax.axis_index("dp") * local_rows
    row_grad = accumulate(
        lax.all_gather(owned, "dp", axis=1, tiled=True), all_row_ids, first_row, local_rows
    )
    partial_squares = jnp.sum(row_grad * row_grad, axis=0)
    squares = lax.psum(partial_squares, "table")
    new_state = adagrad_state + squares / W
    new_table = table_block - learn_rate * row_grad / jnp.sqrt(new_state)[None, :]
    return (new_table, new_state)


def solution(mesh):
    in_specs = (P(None, ("dp", "table")), P(("dp", "table")), P("table", "dp"), P("dp"))
    out_specs = (P("table", "dp"), P("dp"))
    return jax.shard_map(body, mesh=mesh, in_specs=in_specs, out_specs=out_specs, check_vma=False)
```

profile of v0, /device:TPU:8, one launch (start us, length us, event | category | flops | bytes accessed | tf_op | source)
XLA Modules:
  0.0 214.5 jit_solution(18062439507933522561)
XLA Ops:
  7.2 6.3 %all-to-all-start = ((bf16[16,16,128]{2,1,0:T(8,128)(2,1)}), bf16[16,16,128]{2,1,0:T(8,128)(2,1)S(1)}, u32[]{:S(2)}, u32[]{:S(2)}) async-start(bf16[16,16,128]{2,1,0:T(8,128)(2,1)} %bitcast.12), calls=%async_computation | async-start | bytes 131072 | tf_op jit(solution)/shard_map/all_to_all | solution.py:19
  13.4 0.0 all-reduce.2.cloned.1.call-start
  13.5 38.0 %all-gather = s32[32,1,128]{2,1,0:T(1,128)S(1)} all-gather(s32[1,1,128]{2,1,0:T(1,128)} %bitcast.15), channel_id=1, replica_groups=mesh['dp'=2,'table'=16] {'dp','table'}, dimensions={0}, use_global_device_ids=true | all-gather | bytes 16896 | tf_op jit(solution)/shard_map/all_gather | solution.py:21
  51.5 0.0 all-to-all-done
  51.5 0.3 copy.9
  51.8 14.8 %all_gather.7 = bf16[16,4096]{0,1:T(8,128)(2,1)S(1)} all-gather(bf16[16,2048]{0,1:T(8,128)(2,1)S(1)} %bitcast.10), channel_id=1, replica_groups=mesh['dp'=2,'table'=16] {'dp'}, dimensions={1}, use_global_device_ids=true | all-gather | bytes 196608 | tf_op jit(solution)/shard_map/all_gather | solution.py:24
  66.7 0.0 copy-start
  66.7 26.1 %scatter_custom_fusion = f32[16,16384]{0,1:T(8,128)} fusion(s32[4096]{0:T(1024)S(1)} %compare_select_fusion, f32[]{:T(128)} %constant.7.clone.1, bf16[16,4096]{0,1:T(8,128)(2,1)S(1)} %all_gather.7), kind=kCustom, calls=%fused_computation.3 | custom fusion | flops 131072 | bytes 2097156 | tf_op jit(solution)/shard_map/scatter-add | solution.py:15
  92.8 0.0 copy-start.1
  92.8 5.3 %multiply_reduce_fusion = f32[16384]{0:T(1024)} fusion(f32[16,16384]{0,1:T(8,128)} %scatter_custom_fusion), kind=kLoop, calls=%fused_computation.2 | loop fusion | flops 507904 | bytes 1114112 | tf_op jit(solution)/shard_map/reduce_sum | solution.py:26
  98.1 0.0 all-reduce.2.cloned.1.call-update
  98.1 0.0 copy-done
  98.1 4.6 %copy.10 = f32[16,16384]{0,1:T(8,128)} copy(f32[16,16384]{1,0:T(8,128)S(1)} %copy-done) | data formatting | bytes 2097152 | tf_op args[2]
  102.7 84.2 %all-reduce.2.cloned.1.call-done = f32[16384]{0:T(1024)} async-done(((f32[16384]{0:T(1024)}), f32[16384]{0:T(1024)}) %all-reduce.2.cloned.1.call-update) | async-done | bytes 65552 | tf_op jit(solution)/shard_map/psum | solution.py:27
  186.9 0.0 copy-done.1
  186.9 1.5 fusion.4
  188.4 13.3 %divide_subtract_fusion = f32[16,16384]{0,1:T(8,128)} fusion(f32[16,16384]{0,1:T(8,128)} %copy.10, f32[16,16384]{0,1:T(8,128)} %scatter_custom_fusion, f32[16384]{0:T(1024)S(1)} %get-tuple-element.6), kind=kLoop, calls=%fused_computation.1 | loop fusion | flops 786432 | bytes 3211264 | tf_op jit(solution)/shard_map/sub | solution.py:29
  201.7 6.0 %copy.11 = f32[16,16384]{1,0:T(8,128)} copy(f32[16,16384]{0,1:T(8,128)} %divide_subtract_fusion) | data formatting | bytes 2097152
  (2 shorter events, 0.0 us)
Async XLA Ops:
  7.2 44.4 %all-to-all-start = ((bf16[16,16,128]{2,1,0:T(8,128)(2,1)}), bf16[16,16,128]{2,1,0:T(8,128)(2,1)S(1)}, u32[]{:S(2)}, u32[]{:S(2)}) async-start(bf16[16,16,128]{2,1,0:T(8,128)(2,1)} %bitcast.12), calls=%async_computation | async-start | bytes 131072 | tf_op jit(solution)/shard_map/all_to_all | solution.py:19
  13.4 173.5 %all-reduce.2.cloned.1.call-start = ((), (), s32[]{:S(2)}) async-start(), calls=%async_computation.1 | async-start | bytes 131072 | tf_op jit(solution)/shard_map/psum | solution.py:27
  66.7 31.4 %copy-start = (f32[16,16384]{1,0:T(8,128)S(1)}, f32[16,16384]{1,0:T(8,128)}, u32[]{:S(2)}) copy-start(f32[16,16384]{1,0:T(8,128)} %param.6) | copy-start | bytes 3145732
  92.8 94.1 %copy-start.1 = (f32[16384]{0:T(1024)S(1)}, f32[16384]{0:T(1024)}, u32[]{:S(2)}) copy-start(f32[16384]{0:T(1024)} %param.7) | copy-start | bytes 196612
Sparse Core Ops, SparseCore 0:
  98.2 88.6 all-reduce.1
where the time goes:
time: 215 us
  waiting for transfers between devices  84.2 us (39%)
  blocking collectives  52.9 us (25%)
  other arithmetic  46.2 us (21%)
  between operations  14.1 us (7%)
  local copies, waits for them, and re-layouts  10.9 us (5%)
  starting transfers between devices  6.32 us (3%)
    psum x1, waiting for transfers between devices, body(): squares = lax.psum(partial_squares, 'table')  84.2 us
    all_gather x1, blocking collectives, body(): all_row_ids = lax.all_gather(row_ids, ('dp', 'table'), axis=0, tiled=True)  38 us
    scatter-add x1, other arithmetic, accumulate(): return start_total.at[:, target].add(grads.astype(jnp.float32), mode='drop')  26.1 us
    all_gather x1, blocking collectives, body(): lax.all_gather(owned, 'dp', axis=1, tiled=True)  14.8 us
    sub x1, other arithmetic, body(): table_block - learn_rate * row_grad / jnp.sqrt(new_state)[None, :]  13.3 us
    unnamed x6, local copies, waits for them, and re-layouts  10.6 us
    all_to_all x1, starting transfers between devices, body(): lax.all_to_all(gradients, 'table', split_axis=0, concat_axis=1, tiled=True)  6.28 us
    reduce_sum x1, other arithmetic, body(): partial_squares = jnp.sum(row_grad * row_grad, axis=0)  5.28 us
  transfers between devices with their start and end apart: 2, of which 1 were waited for; matrix products, arithmetic and copies ran while one was open for 2% of the time, Pallas kernels for 0%

commit v1 on v0

--- a/solution.py
+++ b/solution.py
@@ -24,7 +24,9 @@
         lax.all_gather(owned, "dp", axis=1, tiled=True), all_row_ids, first_row, local_rows
     )
     partial_squares = jnp.sum(row_grad * row_grad, axis=0)
-    squares = lax.psum(partial_squares, "table")
+    squares = partial_squares
+    for hop in (1, 2, 4, 8):
+        squares = squares + lax.ppermute(squares, "table", [(dev, dev ^ hop) for dev in range(16)])
     new_state = adagrad_state + squares / W
     new_table = table_block - learn_rate * row_grad / jnp.sqrt(new_state)[None, :]
     return (new_table, new_state)

time: 215 us -> 132 us (0.61)
  the two profiles are of different devices: /device:TPU:8 before, /device:TPU:0 now
where the time goes in v1:
time: 132 us; the launch traced here: 131 us
  blocking collectives  56.9 us (43%)
  other arithmetic  44.7 us (34%)
  local copies, waits for them, and re-layouts  10.9 us (8%)
  waiting for transfers between devices  10.4 us (8%)
  starting transfers between devices  7.68 us (6%)
    all_gather x1, blocking collectives, body(): all_row_ids = lax.all_gather(row_ids, ('dp', 'table'), axis=0, tiled=True)  42.1 us
    scatter-add x1, other arithmetic, accumulate(): return start_total.at[:, target].add(grads.astype(jnp.float32), mode='drop')  26.1 us
    all_gather x1, blocking collectives, body(): lax.all_gather(owned, 'dp', axis=1, tiled=True)  14.8 us
    sub x1, other arithmetic, body(): table_block - learn_rate * row_grad / jnp.sqrt(new_state)[None, :]  13.3 us
    unnamed x6, local copies, waits for them, and re-layouts  10.6 us
    ppermute x4, waiting for transfers between devices, body(): lax.ppermute(squares, 'table', [(dev, dev ^ hop) for dev in range(16)])  10.4 us
    all_to_all x1, starting transfers between devices, body(): lax.all_to_all(gradients, 'table', split_axis=0, concat_axis=1, tiled=True)  7.4 us
    reduce_sum x1, other arithmetic, body(): partial_squares = jnp.sum(row_grad * row_grad, axis=0)  4.65 us
  transfers between devices with their start and end apart: 5, of which 4 were waited for; matrix products, arithmetic and copies ran while one was open for 4% of the time, Pallas kernels for 0%

profile of v1, /device:TPU:0, one launch (start us, length us, event | category | flops | bytes accessed | tf_op | source)
XLA Modules:
  0.0 131.3 jit_solution(17381492449079272449)
XLA Ops:
  0.6 7.4 %all-to-all-start = ((bf16[16,16,128]{2,1,0:T(8,128)(2,1)}), bf16[16,16,128]{2,1,0:T(8,128)(2,1)S(1)}, u32[]{:S(2)}, u32[]{:S(2)}) async-start(bf16[16,16,128]{2,1,0:T(8,128)(2,1)} %bitcast.12), calls=%async_computation | async-start | bytes 131072 | tf_op jit(solution)/shard_map/all_to_all | solution.py:19
  8.0 42.1 %all-gather = s32[32,1,128]{2,1,0:T(1,128)S(1)} all-gather(s32[1,1,128]{2,1,0:T(1,128)} %bitcast.15), channel_id=1, replica_groups=mesh['dp'=2,'table'=16] {'dp','table'}, dimensions={0}, use_global_device_ids=true | all-gather | bytes 16896 | tf_op jit(solution)/shard_map/all_gather | solution.py:21
  50.1 0.0 all-to-all-done
  50.1 0.3 copy.9
  50.4 14.8 %all_gather.7 = bf16[16,4096]{0,1:T(8,128)(2,1)S(1)} all-gather(bf16[16,2048]{0,1:T(8,128)(2,1)S(1)} %bitcast.10), channel_id=1, replica_groups=mesh['dp'=2,'table'=16] {'dp'}, dimensions={1}, use_global_device_ids=true | all-gather | bytes 196608 | tf_op jit(solution)/shard_map/all_gather | solution.py:24
  65.2 0.0 copy-start
  65.2 26.1 %scatter_custom_fusion = f32[16,16384]{0,1:T(8,128)} fusion(s32[4096]{0:T(1024)S(1)} %compare_select_fusion, f32[]{:T(128)} %constant.7.clone.1, bf16[16,4096]{0,1:T(8,128)(2,1)S(1)} %all_gather.7), kind=kCustom, calls=%fused_computation.3 | custom fusion | flops 131072 | bytes 2097156 | tf_op jit(solution)/shard_map/scatter-add | solution.py:15
  91.4 0.0 copy-start.1
  91.4 4.6 %multiply_reduce_fusion = f32[16384]{0:T(1024)S(1)} fusion(f32[16,16384]{0,1:T(8,128)} %scatter_custom_fusion), kind=kLoop, calls=%fused_computation.2 | loop fusion | flops 507904 | bytes 1114112 | tf_op jit(solution)/shard_map/reduce_sum | solution.py:26
  96.0 0.1 collective-permute-start
  96.1 1.2 collective-permute-done
  97.3 0.1 collective-permute-start.1
  97.4 4.3 %collective-permute-done.1 = f32[16384]{0:T(1024)S(1)} collective-permute-done((f32[16384]{0:T(1024)S(1)}, f32[16384]{0:T(1024)S(1)}, u32[]{:S(2)}, u32[]{:S(2)}) %collective-permute-start.1) | collective-permute-done | bytes 65568 | tf_op jit(solution)/shard_map/ppermute | solution.py:29
  101.7 0.1 collective-permute-start.2
  101.8 4.3 %collective-permute-done.2 = f32[16384]{0:T(1024)S(1)} collective-permute-done((f32[16384]{0:T(1024)S(1)}, f32[16384]{0:T(1024)S(1)}, u32[]{:S(2)}, u32[]{:S(2)}) %collective-permute-start.2) | collective-permute-done | bytes 65568 | tf_op jit(solution)/shard_map/ppermute | solution.py:29
  106.0 0.1 collective-permute-start.3
  106.1 0.0 copy-done
  106.1 4.6 %copy.10 = f32[16,16384]{0,1:T(8,128)} copy(f32[16,16384]{1,0:T(8,128)S(1)} %copy-done) | data formatting | bytes 2097152 | tf_op args[2]
  110.7 0.7 collective-permute-done.3
  111.4 0.0 copy-done.1
  111.4 0.7 fusion.4
  112.1 13.3 %divide_subtract_fusion = f32[16,16384]{0,1:T(8,128)} fusion(f32[16,16384]{0,1:T(8,128)} %copy.10, f32[16,16384]{0,1:T(8,128)} %scatter_custom_fusion, f32[16384]{0:T(1024)S(1)} %get-tuple-element.6), kind=kLoop, calls=%fused_computation.1 | loop fusion | flops 786432 | bytes 3211264 | tf_op jit(solution)/shard_map/sub | solution.py:31
  125.3 6.0 %copy.11 = f32[16,16384]{1,0:T(8,128)} copy(f32[16,16384]{0,1:T(8,128)} %divide_subtract_fusion) | data formatting | bytes 2097152
  (5 shorter events, 0.0 us)
Async XLA Ops:
  0.6 49.5 %all-to-all-start = ((bf16[16,16,128]{2,1,0:T(8,128)(2,1)}), bf16[16,16,128]{2,1,0:T(8,128)(2,1)S(1)}, u32[]{:S(2)}, u32[]{:S(2)}) async-start(bf16[16,16,128]{2,1,0:T(8,128)(2,1)} %bitcast.12), calls=%async_computation | async-start | bytes 131072 | tf_op jit(solution)/shard_map/all_to_all | solution.py:19
  65.2 40.9 %copy-start = (f32[16,16384]{1,0:T(8,128)S(1)}, f32[16,16384]{1,0:T(8,128)}, u32[]{:S(2)}) copy-start(f32[16,16384]{1,0:T(8,128)} %param.6) | copy-start | bytes 3145732
  91.4 20.1 %copy-start.1 = (f32[16384]{0:T(1024)S(1)}, f32[16384]{0:T(1024)}, u32[]{:S(2)}) copy-start(f32[16384]{0:T(1024)} %param.7) | copy-start | bytes 196612
  96.0 1.3 %collective-permute-start = (f32[16384]{0:T(1024)S(1)}, f32[16384]{0:T(1024)S(1)}, u32[]{:S(2)}, u32[]{:S(2)}) collective-permute-start(f32[16384]{0:T(1024)S(1)} %multiply_reduce_fusion), channel_id=1, source_target_pairs={{0,1},{1,0},{2,3},{3,2},{4,5},{5,4},{6,7},{7,6},{8,9},{9,8},{10,11... | collective-permute-start | bytes 196616 | tf_op jit(solution)/shard_map/ppermute | solution.py:29
  97.3 4.3 %collective-permute-start.1 = (f32[16384]{0:T(1024)S(1)}, f32[16384]{0:T(1024)S(1)}, u32[]{:S(2)}, u32[]{:S(2)}) collective-permute-start(f32[16384]{0:T(1024)S(1)} %add.21), channel_id=1, source_target_pairs={{0,2},{1,3},{2,0},{3,1},{4,6},{5,7},{6,4},{7,5},{8,10},{9,11},{10,... | collective-permute-start | bytes 196616 | tf_op jit(solution)/shard_map/ppermute | solution.py:29
  101.7 4.3 %collective-permute-start.2 = (f32[16384]{0:T(1024)S(1)}, f32[16384]{0:T(1024)S(1)}, u32[]{:S(2)}, u32[]{:S(2)}) collective-permute-start(f32[16384]{0:T(1024)S(1)} %add.22), channel_id=1, source_target_pairs={{0,4},{1,5},{2,6},{3,7},{4,0},{5,1},{6,2},{7,3},{8,12},{9,13},{10,... | collective-permute-start | bytes 196616 | tf_op jit(solution)/shard_map/ppermute | solution.py:29
  106.0 5.4 %collective-permute-start.3 = (f32[16384]{0:T(1024)S(1)}, f32[16384]{0:T(1024)S(1)}, u32[]{:S(2)}, u32[]{:S(2)}) collective-permute-start(f32[16384]{0:T(1024)S(1)} %add.23), channel_id=1, source_target_pairs={{0,8},{1,9},{2,10},{3,11},{4,12},{5,13},{6,14},{7,15},{8,0},{9,1},... | collective-permute-start | bytes 196616 | tf_op jit(solution)/shard_map/ppermute | solution.py:29
